TPU v7x, 32 devices: a whole 2x2x4 slice. The times are simulated.
32 devices in a mesh: slab: 8 (over z, x), depth: 4 (over y, core).
Axes of the slice: x: 2, y: 2, z: 4, core: 2. Of those that a mesh axis runs over, the one named last changes fastest.
Arguments:
- right_side: float32 [3, 8, 8, 32, 256], P(None, None, 'slab', 'depth'), may hold values from -4 to 9
- smoother: float32 [3, 8, 32, 256], P(None, 'slab', 'depth'), may hold values from 0.1 to 1
- material: int32 [8, 32, 256], P('slab', 'depth'), may hold values from 0 to 15
- moduli: float32 [16], replicated, may hold values from 0.25 to 4
- element_matrix: float32 [24, 24], replicated, may hold values from -0.15 to 3, as said below
- coarse_inverse: float32 [24, 24], replicated, may hold values from -0.2 to 1.2, as said below
- surface_map: int32 [8, 256], P('slab'), may hold values from 0 to 2047, as said below
- line_of_sight: float32 [3, 8, 256], P(None, 'slab'), may hold values from -3 to 3
Outputs:
- residual: float32 [3, 8, 8, 32, 256], P(None, None, 'slab', 'depth')
- pixels: float32 [8, 2048], P('depth', 'slab')
Inputs may be any that keep to these rules, and one draw needn't show every extreme that they name: `element_matrix`: symmetric. `coarse_inverse`: symmetric. `surface_map`: pixel p lies in tile p // 256. At most 64 surface nodes of one slab block lie in one tile, and some tile holds exactly 64 surface nodes of every slab block.
All inputs are finite; a program needn't handle non-finite values.
Results may differ from a plain program's by a relative error of at most 0.0003.
Values sent between devices are 32-bit elements; how exact they have to be, the bound alone decides.
No kernel may reach another device: no remote copies, remote signals or barrier semaphores. Data moves between devices by JAX's collectives and lax.ppermute only.
A program may use at most 64 MiB of HBM per device.

v0:
```python
import jax
import jax.numpy as jnp
from jax import lax
from jax.sharding import PartitionSpec as P

PIX = 256


def extended(array, sides, width):
    for axis, dim in sides:
        peers, length = (lax.axis_size(axis), array.shape[dim])
        up = [(i, (i + 1) % peers) for i in range(peers - 1)]
        down = [(j, i) for i, j in up]
        last = lax.slice_in_dim(array, length - width, length, axis=dim)
        initial = lax.slice_in_dim(array, 0, width, axis=dim)
        before = lax.ppermute(last, axis, up)
        after = lax.ppermute(initial, axis, down)
        array = jnp.concatenate([before, array, after], axis=dim)
    return array


def broadcast(value, axis, source):
    kept = jnp.where(lax.axis_index(axis) == source, value, 0).astype(value.dtype)
    return lax.psum(kept, axis)


def stiffness(padded_field, padded_moduli, element_matrix):
    sources = padded_field.shape[1]
    span_x = padded_field.shape[2] - 1
    span_z = padded_field.shape[3] - 1
    span_y = padded_moduli.shape[2]
    corners = []
    for corner in range(8):
        along_x, along_z, along_y = (corner // 4, corner // 2 % 2, corner % 2)
        corners.append(
            padded_field[
                :,
                :,
                along_x : along_x + span_x,
                along_z : along_z + span_z,
                along_y : along_y + span_y,
            ]
        )
    stacked = jnp.stack(corners, 0).reshape(24, -1)
    forces = jnp.dot(
        element_matrix, stacked, precision=lax.Precision.HIGHEST, preferred_element_type=jnp.float32
    )
    forces = forces.reshape(8, 3, sources, span_x, span_z, span_y) * padded_moduli[1:, 1:, :]
    forces = jnp.pad(forces, ((0, 0), (0, 0), (0, 0), (0, 0), (0, 0), (0, 1)))
    summed = jnp.zeros((3, sources, span_x - 1, span_z - 1, span_y), jnp.float32)
    for corner in range(8):
        along_x, along_z, along_y = (corner // 4, corner // 2 % 2, corner % 2)
        summed = (
            summed
            + forces[
                corner,
                :,
                :,
                1 - along_x : 1 - along_x + span_x - 1,
                1 - along_z : 1 - along_z + span_z - 1,
                1 - along_y : 1 - along_y + span_y,
            ]
        )
    return summed


def pack_slots(values, targets, n_slab):
    node_count = values.shape[1]
    capacity = 2 * node_count // n_slab
    tile_owner = targets // PIX
    in_tile = targets % PIX
    onehot = (tile_owner[:, None] == jnp.arange(n_slab, dtype=jnp.int32)[None]).astype(jnp.int32)
    slot_rank = jnp.sum((jnp.cumsum(onehot, axis=0) - 1) * onehot, axis=1)
    send_vals = (
        jnp.zeros((values.shape[0], capacity, n_slab), jnp.float32)
        .at[:, slot_rank, tile_owner]
        .set(values)
    )
    send_ids = (
        jnp.zeros((1, capacity, n_slab), jnp.float32)
        .at[0, slot_rank, tile_owner]
        .set(in_tile.astype(jnp.float32))
    )
    return (send_vals, send_ids)


def bin_pixels(got_vals, got_ids):
    pixel_index = got_ids.reshape(-1).astype(jnp.int32)
    rows = got_vals.shape[0]
    return jnp.zeros((rows, PIX), jnp.float32).at[:, pixel_index].add(got_vals.reshape(rows, -1))


def body(
    right_side,
    smoother,
    material,
    moduli,
    element_matrix,
    coarse_inverse,
    surface_map,
    line_of_sight,
):
    components, sources, width_x, width_z, width_y = right_side.shape
    n_slab = lax.axis_size("slab")
    n_depth = lax.axis_size("depth")
    slab_rank = lax.axis_index("slab")
    depth_rank = lax.axis_index("depth")
    levels = jnp.arange(moduli.shape[0], dtype=jnp.int32)
    modulus_field = jnp.sum(
        jnp.where(material[None] == levels[:, None, None, None], moduli[:, None, None, None], 0.0),
        axis=0,
    )
    weights = smoother[:, None]
    stacked = jnp.concatenate(
        [
            right_side.reshape(components * sources, width_x, width_z, width_y),
            smoother,
            modulus_field[None],
        ],
        0,
    )
    source_pad = extended(stacked, (("slab", 1), ("depth", 2)), 1)
    agg_nodes = float(width_x * width_z * n_depth * width_y)
    block_sums = jnp.sum(right_side, axis=(2, 3, 4))
    placed = jnp.where(
        jnp.arange(n_slab, dtype=jnp.int32)[:, None, None] == slab_rank, block_sums[None], 0.0
    )
    placed = placed.reshape(components * n_slab, sources)
    coarse_sum = lax.psum(placed, ("slab", "depth"))
    coarse_vec = coarse_sum / agg_nodes
    correction = jnp.dot(
        coarse_inverse,
        coarse_vec,
        precision=lax.Precision.HIGHEST,
        preferred_element_type=jnp.float32,
    )
    by_block = correction.reshape(n_slab, components, sources)
    own_corr = lax.dynamic_index_in_dim(by_block, slab_rank, 0, keepdims=False)
    direction = weights * right_side + own_corr[:, :, None, None, None]
    numerator = lax.psum(jnp.sum(right_side * direction, axis=(0, 2, 3, 4)), ("slab", "depth"))
    field_pad = source_pad[: components * sources].reshape(
        components, sources, width_x + 2, width_z + 2, width_y
    )
    weight_pad = source_pad[components * sources : components * sources + components]
    moduli_pad = source_pad[components * sources + components]
    low_block = jnp.maximum(slab_rank - 1, 0)
    high_block = jnp.minimum(slab_rank + 1, n_slab - 1)
    low_corr = jnp.where(
        slab_rank > 0, lax.dynamic_index_in_dim(by_block, low_block, 0, keepdims=False), 0.0
    )
    high_corr = jnp.where(
        slab_rank < n_slab - 1,
        lax.dynamic_index_in_dim(by_block, high_block, 0, keepdims=False),
        0.0,
    )
    row_corr = jnp.concatenate([low_corr[None], own_corr[None], high_corr[None]], 0)
    row_corr = jnp.transpose(row_corr, (1, 2, 0))
    depth_mask = jnp.ones((width_z + 2,), jnp.float32)
    depth_mask = depth_mask.at[0].set(jnp.where(depth_rank > 0, 1.0, 0.0))
    depth_mask = depth_mask.at[width_z + 1].set(jnp.where(depth_rank < n_depth - 1, 1.0, 0.0))
    padded = (
        weight_pad[:, None] * field_pad
        + row_corr[:, :, :, None, None] * depth_mask[None, None, None, :, None]
    )
    padded = jnp.pad(padded, ((0, 0), (0, 0), (0, 0), (0, 0), (1, 0)))
    applied = stiffness(padded, moduli_pad, element_matrix)
    denominator = lax.psum(jnp.sum(direction * applied, axis=(0, 2, 3, 4)), ("slab", "depth"))
    step_size = numerator / denominator
    residual = right_side - step_size[None, :, None, None, None] * applied
    surface = step_size[None, :, None, None] * direction[:, :, :, width_z - 1, :]
    projected = jnp.sum(line_of_sight[:, None] * surface, axis=0).reshape(sources, -1)
    projected = broadcast(projected, "depth", n_depth - 1)
    targets = surface_map.reshape(-1)
    per_row = sources // n_depth
    send_vals, send_ids = pack_slots(projected, targets, n_slab)
    got_vals, got_ids = (
        lax.all_to_all(send_vals, "slab", split_axis=2, concat_axis=2, tiled=True),
        lax.all_to_all(send_ids, "slab", split_axis=2, concat_axis=2, tiled=True),
    )
    binned = bin_pixels(got_vals, got_ids)
    pixels = lax.dynamic_slice_in_dim(binned, depth_rank * per_row, per_row, 0)
    return (residual, pixels)


def solution(mesh):
    return jax.shard_map(
        body,
        mesh=mesh,
        in_specs=(
            P(None, None, "slab", "depth", None),
            P(None, "slab", "depth", None),
            P("slab", "depth", None),
            P(),
            P(),
            P(),
            P("slab", None),
            P(None, "slab", None),
        ),
        out_specs=(P(None, None, "slab", "depth", None), P("depth", "slab")),
        check_vma=False,
    )
```

profile of v0, /device:TPU:0, one launch (start us, length us, event | category | flops | bytes accessed | tf_op | source)
XLA Modules:
  0.0 215.8 jit_solution(9086493570849835887)
XLA Ops:
  0.7 0.8 select_reduce_fusion
  1.5 1.0 pad_maximum_fusion.1
  2.5 1.3 collective-permute-start.1
  3.8 5.5 %collective-permute-start = (f32[28,1,8,256]{3,2,1,0:T(8,128)S(1)}, f32[28,1,8,256]{3,2,1,0:T(8,128)S(1)}, u32[]{:S(2)}, u32[]{:S(2)}) collective-permute-start(f32[28,1,8,256]{3,2,1,0:T(8,128)S(1)} %pad_maximum_fusion.1), channel_id=1, source_target_pairs={{0,4},{4,8},{8,12},{12,16},{16,20},{20,24},{24,28},{1,5},{5,9},{9,... | collective-permute-start | bytes 688136 | tf_op jit(solution)/shard_map/ppermute | solution.py:16
  12.9 38.7 %scatter_fusion = f32[64,8]{0,1:T(8,128)} fusion(f32[64,8]{0,1:T(8,128)} %broadcast.316, s32[256]{0:T(256)S(1)} %bitcast.120, f32[256]{0:T(256)S(1)} %get-tuple-element.49), kind=kCustom, calls=%fused_computation | custom fusion | bytes 5120 | tf_op jit(solution)/shard_map/scatter | solution.py:82
  51.6 6.2 %all-to-all-start = ((f32[1,64,8]{1,0,2:T(1,128)}), f32[1,64,8]{1,0,2:T(1,128)S(1)}, u32[]{:S(2)}, u32[]{:S(2)}) async-start(f32[1,64,8]{1,0,2:T(1,128)} %bitcast.34), calls=%async_computation | async-start | bytes 8192 | tf_op jit(solution)/shard_map/all_to_all | solution.py:178
  57.8 1.1 reduce_sum.56
  59.2 40.8 %psum.28 = f32[24,8]{1,0:T(8,128)S(1)} all-reduce(f32[24,8]{1,0:T(8,128)S(1)} %broadcast_select_fusion), channel_id=1, replica_groups=mesh['slab'=8,'depth'=4] {'slab','depth'}, use_global_device_ids=true, to_apply=%region_1.2 | all-reduce | flops 192 | bytes 1536 | tf_op jit(solution)/shard_map/psum | solution.py:129
  100.0 0.9 convolution_bitcast_fusion.1
  101.7 1.3 copy.99
  103.2 0.9 pad_maximum_fusion.7
  104.1 1.3 collective-permute-start.2
  105.4 1.3 collective-permute-start.3
  107.3 3.9 %collective-permute-done.3 = f32[28,3,1,256]{3,2,1,0:T(1,128)S(1)} collective-permute-done((f32[28,3,1,256]{3,2,1,0:T(1,128)S(1)}, f32[28,3,1,256]{3,2,1,0:T(1,128)S(1)}, u32[]{:S(2)}, u32[]{:S(2)}) %collective-permute-start.3) | collective-permute-done | bytes 86048 | tf_op jit(solution)/shard_map/ppermute | solution.py:17
  112.4 1.1 fusion.1
  113.6 1.0 fusion.11
  114.6 1.2 fusion.3
  115.7 1.0 fusion.10
  116.7 1.1 fusion.5
  117.9 0.9 fusion.9
  118.8 1.2 fusion.7
  120.0 1.0 fusion.8
  121.0 3.8 %reshape.438 = f32[24,36864]{1,0:T(8,128)S(1)} reshape(f32[8,3,8,2,9,256]{5,4,3,2,1,0:T(8,128)} %fusion.8) | data formatting | bytes 7077888 | tf_op jit(solution)/shard_map/reshape | solution.py:44
  124.8 4.9 %convolution_bitcast_fusion = f32[24,36864]{1,0:T(8,128)} fusion(f32[24,36864]{1,0:T(8,128)S(1)} %reshape.438, f32[24,24]{1,0:T(8,128)S(1)} %copy-done), kind=kOutput, calls=%fused_computation.3 | convolution fusion | flops 254803968 | bytes 7080192 | tf_op jit(solution)/shard_map/dot_general | solution.py:45
  129.8 5.2 %reshape.439 = f32[8,3,8,2,9,256]{5,4,3,2,1,0:T(8,128)} reshape(f32[24,36864]{1,0:T(8,128)} %convolution_bitcast_fusion) | data formatting | bytes 7077888 | tf_op jit(solution)/shard_map/reshape | solution.py:48
  135.0 3.6 %broadcast_multiply_fusion = f32[8,3,8,2,9,256]{5,4,3,2,1,0:T(8,128)S(1)} fusion(f32[8,3,8,2,9,256]{5,4,3,2,1,0:T(8,128)} %reshape.439, f32[2,9,256]{2,1,0:T(8,128)S(1)} %copy-done.5), kind=kLoop, calls=%fused_computation.8 | loop fusion | flops 884736 | bytes 7096320 | tf_op jit(solution)/shard_map/mul | solution.py:48
  139.1 40.8 %all-reduce.3 = (f32[8]{0:T(128)S(1)}, f32[8]{0:T(128)S(1)}) all-reduce(f32[8]{0:T(128)S(1)} %get-tuple-element.39, f32[8]{0:T(128)S(1)} %get-tuple-element.38), channel_id=1, replica_groups=mesh['slab'=8,'depth'=4] {'slab','depth'}, use_global_device_ids=true, to_apply=%region_3.4 | all-reduce | flops 16 | bytes 128 | tf_op jit(solution)/shard_map/psum | solution.py:140
  180.1 6.7 %psum.31 = f32[8,256]{1,0:T(8,128)S(1)} all-reduce(f32[8,256]{1,0:T(8,128)S(1)} %broadcast_select_fusion.1), channel_id=1, replica_groups=mesh['slab'=8,'depth'=4] {'depth'}, use_global_device_ids=true, to_apply=%region_12.13 | all-reduce | flops 2048 | bytes 16384 | tf_op jit(solution)/shard_map/psum | solution.py:24
  187.0 11.6 %scatter_fusion.1 = f32[8,64,8]{0,2,1:T(8,128)S(1)} fusion(f32[8,64,8]{0,2,1:T(8,128)S(1)} %broadcast_in_dim.103, s32[256]{0:T(256)S(1)} %bitcast.121, f32[256,8]{1,0:T(8,128)S(1)} %copy.81), kind=kCustom, calls=%fused_computation.1 | custom fusion | bytes 26624 | tf_op jit(solution)/shard_map/scatter | solution.py:77
  199.5 4.3 %all-to-all-start.1 = ((f32[8,1,512]{2,1,0:T(1,128)}), f32[8,1,512]{2,1,0:T(1,128)S(1)}, u32[]{:S(2)}, u32[]{:S(2)}) async-start(f32[8,1,512]{2,1,0:T(1,128)} %reshape.473), calls=%async_computation.1 | async-start | bytes 32768 | tf_op jit(solution)/shard_map/all_to_all | solution.py:177
  204.5 5.8 %all-to-all-done.1 = f32[8,1,512]{2,1,0:T(1,128)S(1)} async-done(((f32[8,1,512]{2,1,0:T(1,128)}), f32[8,1,512]{2,1,0:T(1,128)S(1)}, u32[]{:S(2)}, u32[]{:S(2)}) %all-to-all-start.1) | async-done | bytes 16416 | tf_op jit(solution)/shard_map/all_to_all | solution.py:177
  212.1 2.9 %scatter_custom_fusion.2 = f32[8,256]{0,1:T(8,128)S(1)} fusion(s32[512]{0:T(512)} %bitcast.145, f32[512,8]{1,0:T(8,128)S(1)} %copy.85, f32[]{:T(128)} %constant.114.clone.1), kind=kCustom, calls=%fused_computation.57 | custom fusion | flops 4096 | bytes 8704 | tf_op jit(solution)/shard_map/scatter-add | solution.py:90
  (73 shorter events, 11.3 us)
Async XLA Ops:
  0.6 124.2 %copy-start = (f32[24,24]{1,0:T(8,128)S(1)}, f32[24,24]{1,0:T(8,128)}, u32[]{:S(2)}) copy-start(f32[24,24]{1,0:T(8,128)} %param.16) | copy-start | bytes 6916
  0.6 110.5 %copy-start.3 = (f32[3,1,8,256]{3,2,1,0:T(8,128)S(1)}, f32[3,1,8,256]{3,2,1,0:T(8,128)}, u32[]{:S(2)}) copy-start(f32[3,1,8,256]{3,2,1,0:T(8,128)} %param.13) | copy-start | bytes 73732
  0.7 102.6 %copy-start.1 = (f32[3,8,1,8,256]{4,3,2,1,0:T(8,128)S(1)}, f32[3,8,1,8,256]{4,3,2,1,0:T(8,128)}, u32[]{:S(2)}) copy-start(f32[3,8,1,8,256]{4,3,2,1,0:T(8,128)} %param.12) | copy-start | bytes 589828
  2.5 100.7 %collective-permute-start.1 = (f32[28,1,8,256]{3,2,1,0:T(8,128)S(1)}, f32[28,1,8,256]{3,2,1,0:T(8,128)S(1)}, u32[]{:S(2)}, u32[]{:S(2)}) collective-permute-start(f32[28,1,8,256]{3,2,1,0:T(8,128)S(1)} %pad_maximum_fusion.1), channel_id=1, source_target_pairs={{4,0},{8,4},{12,8},{16,12},{20,16},{24,20},{28,24},{5,1},{9,5},{13... | collective-permute-start | bytes 688136 | tf_op jit(solution)/shard_map/ppermute | solution.py:17
  3.8 99.4 %collective-permute-start = (f32[28,1,8,256]{3,2,1,0:T(8,128)S(1)}, f32[28,1,8,256]{3,2,1,0:T(8,128)S(1)}, u32[]{:S(2)}, u32[]{:S(2)}) collective-permute-start(f32[28,1,8,256]{3,2,1,0:T(8,128)S(1)} %pad_maximum_fusion.1), channel_id=1, source_target_pairs={{0,4},{4,8},{8,12},{12,16},{16,20},{20,24},{24,28},{1,5},{5,9},{9,... | collective-permute-start | bytes 688136 | tf_op jit(solution)/shard_map/ppermute | solution.py:16
  51.6 51.4 %all-to-all-start = ((f32[1,64,8]{1,0,2:T(1,128)}), f32[1,64,8]{1,0,2:T(1,128)S(1)}, u32[]{:S(2)}, u32[]{:S(2)}) async-start(f32[1,64,8]{1,0,2:T(1,128)} %bitcast.34), calls=%async_computation | async-start | bytes 8192 | tf_op jit(solution)/shard_map/all_to_all | solution.py:178
  101.0 0.6 copy-start.6
  104.1 3.1 %collective-permute-start.2 = (f32[28,3,1,256]{3,2,1,0:T(1,128)S(1)}, f32[28,3,1,256]{3,2,1,0:T(1,128)S(1)}, u32[]{:S(2)}, u32[]{:S(2)}) collective-permute-start(f32[28,3,1,256]{3,2,1,0:T(1,128)S(1)} %get-tuple-element.43), channel_id=1, source_target_pairs={{0,1},{1,2},{2,3},{4,5},{5,6},{6,7},{8,9},{9,10},{10,11},{12,13},{... | collective-permute-start | bytes 258056 | tf_op jit(solution)/shard_map/ppermute | solution.py:16
  105.4 5.7 %collective-permute-start.3 = (f32[28,3,1,256]{3,2,1,0:T(1,128)S(1)}, f32[28,3,1,256]{3,2,1,0:T(1,128)S(1)}, u32[]{:S(2)}, u32[]{:S(2)}) collective-permute-start(f32[28,3,1,256]{3,2,1,0:T(1,128)S(1)} %get-tuple-element.44), channel_id=1, source_target_pairs={{1,0},{2,1},{3,2},{5,4},{6,5},{7,6},{9,8},{10,9},{11,10},{13,12},{... | collective-permute-start | bytes 258056 | tf_op jit(solution)/shard_map/ppermute | solution.py:17
  129.8 5.2 %copy-start.5 = (f32[2,9,256]{2,1,0:T(8,128)S(1)}, f32[2,9,256]{2,1,0:T(8,128)}, u32[]{:S(2)}) copy-start(f32[2,9,256]{2,1,0:T(8,128)} %slice.139) | copy-start | bytes 55300
  135.0 3.7 %copy-start.2 = (f32[3,8,1,8,256]{4,3,2,1,0:T(8,128)S(1)}, f32[3,8,1,8,256]{4,3,2,1,0:T(8,128)}, u32[]{:S(2)}) copy-start(f32[3,8,1,8,256]{4,3,2,1,0:T(8,128)} %param.12) | copy-start | bytes 589828
  135.0 3.7 %copy-start.4 = (f32[3,1,8,256]{3,2,1,0:T(8,128)S(1)}, f32[3,1,8,256]{3,2,1,0:T(8,128)}, u32[]{:S(2)}) copy-start(f32[3,1,8,256]{3,2,1,0:T(8,128)} %param.13) | copy-start | bytes 73732
  135.0 3.7 %copy-start.7 = (f32[1,3,8]{2,1,0:T(4,128)S(1)}, f32[1,3,8]{2,1,0:T(4,128)}, u32[]{:S(2)}) copy-start(f32[1,3,8]{2,1,0:T(4,128)} %copy-done.6) | copy-start | bytes 292
  138.7 41.3 %copy-start.8 = (f32[3,1,256]{2,0,1:T(4,128)S(1)}, f32[3,1,256]{2,0,1:T(4,128)}, u32[]{:S(2)}) copy-start(f32[3,1,256]{2,0,1:T(4,128)} %copy.99) | copy-start | bytes 9220
  199.5 10.8 %all-to-all-start.1 = ((f32[8,1,512]{2,1,0:T(1,128)}), f32[8,1,512]{2,1,0:T(1,128)S(1)}, u32[]{:S(2)}, u32[]{:S(2)}) async-start(f32[8,1,512]{2,1,0:T(1,128)} %reshape.473), calls=%async_computation.1 | async-start | bytes 32768 | tf_op jit(solution)/shard_map/all_to_all | solution.py:177
where the time goes:
time: 218 us; the launch traced here: 216 us
  blocking collectives  88.4 us (41%)
  local copies, waits for them, and re-layouts  74.5 us (34%)
  starting transfers between devices  19.9 us (9%)
  other arithmetic  16.4 us (8%)
  waiting for transfers between devices  9.68 us (4%)
  matrix products  5.84 us (3%)
    psum x1, blocking collectives, body(): lax.psum(jnp.sum(right_side * direction, axis=(0, 2, 3, 4)), ('slab', 'de...  40.8 us
    psum x1, blocking collectives, body(): coarse_sum = lax.psum(placed, ('slab', 'depth'))  40.8 us
    scatter x1, local copies, waits for them, and re-layouts, pack_slots(): send_ids = jnp.zeros((1, capacity, n_slab), jnp.float32).at[0, slot_rank,...  38.7 us
    scatter x2, local copies, waits for them, and re-layouts, pack_slots(): send_vals = jnp.zeros((values.shape[0], capacity, n_slab), jnp.float32).a...  11.8 us
    unnamed x29, local copies, waits for them, and re-layouts  10.8 us
    ppermute x2, starting transfers between devices, extended(): before = lax.ppermute(last, axis, up)  6.81 us
    psum x1, blocking collectives, broadcast(): return lax.psum(kept, axis)  6.75 us
    all_to_all x1, starting transfers between devices, body(): lax.all_to_all(send_ids, 'slab', split_axis=2, concat_axis=2, tiled=True)  6.2 us
  transfers between devices with their start and end apart: 6, of which 2 were waited for; matrix products, arithmetic and copies ran while one was open for 22% of the time, Pallas kernels for 0%

commit v1 on v0

--- a/solution.py
+++ b/solution.py
@@ -126,7 +126,8 @@
         jnp.arange(n_slab, dtype=jnp.int32)[:, None, None] == slab_rank, block_sums[None], 0.0
     )
     placed = placed.reshape(components * n_slab, sources)
-    coarse_sum = lax.psum(placed, ("slab", "depth"))
+    parts = lax.all_gather(placed, ("slab", "depth"))
+    coarse_sum = jnp.sum(parts, axis=0)
     coarse_vec = coarse_sum / agg_nodes
     correction = jnp.dot(
         coarse_inverse,

time: 218 us -> 213 us (0.977)
  waiting for transfers between devices: 9.68 us -> 7.16 us
    all_gather x0 -> x1, blocking collectives: none -> 42.3 us  [body(): parts = lax.all_gather(placed, ('slab', 'depth'))]
    psum x1 -> x0, blocking collectives: 40.8 us -> none  [body(): coarse_sum = lax.psum(placed, ('slab', 'depth'))]
    psum x1, blocking collectives: 40.8 us -> 37.5 us  [body(): lax.psum(jnp.sum(right_side * direction, axis=(0, 2, 3, 4)), ('slab', 'de...]
    ppermute x2, waiting for transfers between devices: 3.86 us -> 1.34 us  [extended(): after = lax.ppermute(initial, axis, down)]
    unnamed x29 -> x31, local copies, waits for them, and re-layouts: 10.8 us -> 10.1 us
where the time goes in v1:
time: 213 us; the launch traced here: 212 us
  blocking collectives  87 us (41%)
  local copies, waits for them, and re-layouts  73.9 us (35%)
  starting transfers between devices  21 us (10%)
  other arithmetic  15.7 us (7%)
  waiting for transfers between devices  7.16 us (3%)
  matrix products  5.78 us (3%)
    all_gather x1, blocking collectives, body(): parts = lax.all_gather(placed, ('slab', 'depth'))  42.3 us
    scatter x1, local copies, waits for them, and re-layouts, pack_slots(): send_ids = jnp.zeros((1, capacity, n_slab), jnp.float32).at[0, slot_rank,...  38.7 us
    psum x1, blocking collectives, body(): lax.psum(jnp.sum(right_side * direction, axis=(0, 2, 3, 4)), ('slab', 'de...  37.5 us
    scatter x2, local copies, waits for them, and re-layouts, pack_slots(): send_vals = jnp.zeros((values.shape[0], capacity, n_slab), jnp.float32).a...  11.8 us
    unnamed x31, local copies, waits for them, and re-layouts  10.1 us
    ppermute x2, starting transfers between devices, extended(): before = lax.ppermute(last, axis, up)  7.77 us
    psum x1, blocking collectives, broadcast(): return lax.psum(kept, axis)  7.21 us
    all_to_all x1, starting transfers between devices, body(): lax.all_to_all(send_ids, 'slab', split_axis=2, concat_axis=2, tiled=True)  6.2 us
  transfers between devices with their start and end apart: 6, of which 2 were waited for; matrix products, arithmetic and copies ran while one was open for 22% of the time, Pallas kernels for 0%

profile of v1, /device:TPU:0, one launch (start us, length us, event | category | flops | bytes accessed | tf_op | source)
XLA Modules:
  0.0 211.6 jit_solution(544142934179366257)
XLA Ops:
  0.7 0.8 select_reduce_fusion
  1.5 1.0 pad_maximum_fusion.1
  2.5 1.3 collective-permute-start.1
  3.8 5.5 %collective-permute-start = (f32[28,1,8,256]{3,2,1,0:T(8,128)S(1)}, f32[28,1,8,256]{3,2,1,0:T(8,128)S(1)}, u32[]{:S(2)}, u32[]{:S(2)}) collective-permute-start(f32[28,1,8,256]{3,2,1,0:T(8,128)S(1)} %pad_maximum_fusion.1), channel_id=1, source_target_pairs={{0,4},{4,8},{8,12},{12,16},{16,20},{20,24},{24,28},{1,5},{5,9},{9,... | collective-permute-start | bytes 688136 | tf_op jit(solution)/shard_map/ppermute | solution.py:16
  11.6 0.7 or_select_fusion
  12.9 38.7 %scatter_fusion = f32[64,8]{0,1:T(8,128)} fusion(f32[64,8]{0,1:T(8,128)} %broadcast.335, s32[256]{0:T(256)S(1)} %bitcast.120, f32[256]{0:T(256)S(1)} %get-tuple-element.51), kind=kCustom, calls=%fused_computation | custom fusion | bytes 5120 | tf_op jit(solution)/shard_map/scatter | solution.py:82
  51.6 6.2 %all-to-all-start = ((f32[1,64,8]{1,0,2:T(1,128)}), f32[1,64,8]{1,0,2:T(1,128)S(1)}, u32[]{:S(2)}, u32[]{:S(2)}) async-start(f32[1,64,8]{1,0,2:T(1,128)} %bitcast.34), calls=%async_computation | async-start | bytes 8192 | tf_op jit(solution)/shard_map/all_to_all | solution.py:179
  57.8 1.1 reduce_sum.65
  59.3 42.3 %all_gather.3 = f32[32,24,8]{1,2,0:T(8,128)S(1)} all-gather(f32[1,24,8]{1,2,0:T(8,128)S(1)} %copy.93), channel_id=1, replica_groups=mesh['slab'=8,'depth'=4] {'slab','depth'}, dimensions={0}, use_global_device_ids=true | all-gather | bytes 25344 | tf_op jit(solution)/shard_map/all_gather | solution.py:129
  101.6 0.8 convolution_bitcast_fusion.1
  104.2 2.3 %collective-permute-start.2 = (f32[28,3,1,256]{3,2,1,0:T(1,128)S(1)}, f32[28,3,1,256]{3,2,1,0:T(1,128)S(1)}, u32[]{:S(2)}, u32[]{:S(2)}) collective-permute-start(f32[28,3,1,256]{3,2,1,0:T(1,128)S(1)} %get-tuple-element.45), channel_id=1, source_target_pairs={{0,1},{1,2},{2,3},{4,5},{5,6},{6,7},{8,9},{9,10},{10,11},{12,13},{... | collective-permute-start | bytes 258056 | tf_op jit(solution)/shard_map/ppermute | solution.py:16
  106.5 1.3 collective-permute-start.3
  108.3 1.3 collective-permute-done.3
  110.9 1.1 fusion.1
  112.1 1.0 fusion.11
  113.1 1.2 fusion.3
  114.2 1.0 fusion.10
  115.2 1.1 fusion.5
  116.4 0.9 fusion.9
  117.3 1.2 fusion.7
  118.5 1.0 fusion.8
  119.5 3.8 %reshape.469 = f32[24,36864]{1,0:T(8,128)S(1)} reshape(f32[8,3,8,2,9,256]{5,4,3,2,1,0:T(8,128)} %fusion.8) | data formatting | bytes 7077888 | tf_op jit(solution)/shard_map/reshape | solution.py:44
  123.3 4.9 %convolution_bitcast_fusion = f32[24,36864]{1,0:T(8,128)} fusion(f32[24,36864]{1,0:T(8,128)S(1)} %reshape.469, f32[24,24]{1,0:T(8,128)S(1)} %copy-done), kind=kOutput, calls=%fused_computation.3 | convolution fusion | flops 254803968 | bytes 7080192 | tf_op jit(solution)/shard_map/dot_general | solution.py:45
  128.3 5.2 %reshape.470 = f32[8,3,8,2,9,256]{5,4,3,2,1,0:T(8,128)} reshape(f32[24,36864]{1,0:T(8,128)} %convolution_bitcast_fusion) | data formatting | bytes 7077888 | tf_op jit(solution)/shard_map/reshape | solution.py:48
  133.5 3.6 %broadcast_multiply_fusion = f32[8,3,8,2,9,256]{5,4,3,2,1,0:T(8,128)S(1)} fusion(f32[8,3,8,2,9,256]{5,4,3,2,1,0:T(8,128)} %reshape.470, f32[2,9,256]{2,1,0:T(8,128)S(1)} %copy-done.5), kind=kLoop, calls=%fused_computation.8 | loop fusion | flops 884736 | bytes 7096320 | tf_op jit(solution)/shard_map/mul | solution.py:48
  137.6 37.5 %all-reduce.3 = (f32[8]{0:T(128)S(1)}, f32[8]{0:T(128)S(1)}) all-reduce(f32[8]{0:T(128)S(1)} %get-tuple-element.41, f32[8]{0:T(128)S(1)} %get-tuple-element.40), channel_id=1, replica_groups=mesh['slab'=8,'depth'=4] {'slab','depth'}, use_global_device_ids=true, to_apply=%region_3.4 | all-reduce | flops 16 | bytes 128 | tf_op jit(solution)/shard_map/psum | solution.py:141
  175.2 7.2 %psum.23 = f32[8,256]{1,0:T(8,128)S(1)} all-reduce(f32[8,256]{1,0:T(8,128)S(1)} %broadcast_select_fusion.1), channel_id=1, replica_groups=mesh['slab'=8,'depth'=4] {'depth'}, use_global_device_ids=true, to_apply=%region_12.13 | all-reduce | flops 2048 | bytes 16384 | tf_op jit(solution)/shard_map/psum | solution.py:24
  182.6 11.6 %scatter_fusion.1 = f32[8,64,8]{0,2,1:T(8,128)S(1)} fusion(f32[8,64,8]{0,2,1:T(8,128)S(1)} %broadcast_in_dim.103, s32[256]{0:T(256)S(1)} %bitcast.121, f32[256,8]{1,0:T(8,128)S(1)} %copy.102), kind=kCustom, calls=%fused_computation.1 | custom fusion | bytes 26624 | tf_op jit(solution)/shard_map/scatter | solution.py:77
  195.1 4.5 %all-to-all-start.1 = ((f32[8,1,512]{2,1,0:T(1,128)}), f32[8,1,512]{2,1,0:T(1,128)S(1)}, u32[]{:S(2)}, u32[]{:S(2)}) async-start(f32[8,1,512]{2,1,0:T(1,128)} %reshape.504), calls=%async_computation.1 | async-start | bytes 32768 | tf_op jit(solution)/shard_map/all_to_all | solution.py:178
  199.6 0.8 fusion.21
  200.3 5.8 %all-to-all-done.1 = f32[8,1,512]{2,1,0:T(1,128)S(1)} async-done(((f32[8,1,512]{2,1,0:T(1,128)}), f32[8,1,512]{2,1,0:T(1,128)S(1)}, u32[]{:S(2)}, u32[]{:S(2)}) %all-to-all-start.1) | async-done | bytes 16416 | tf_op jit(solution)/shard_map/all_to_all | solution.py:178
  207.9 2.9 %scatter_custom_fusion.2 = f32[8,256]{0,1:T(8,128)S(1)} fusion(s32[512]{0:T(512)} %bitcast.145, f32[512,8]{1,0:T(8,128)S(1)} %copy.106, f32[]{:T(128)} %constant.114.clone.1), kind=kCustom, calls=%fused_computation.57 | custom fusion | flops 4096 | bytes 8704 | tf_op jit(solution)/shard_map/scatter-add | solution.py:90
  (77 shorter events, 10.7 us)
Async XLA Ops:
  0.6 122.7 %copy-start = (f32[24,24]{1,0:T(8,128)S(1)}, f32[24,24]{1,0:T(8,128)}, u32[]{:S(2)}) copy-start(f32[24,24]{1,0:T(8,128)} %param.16) | copy-start | bytes 6916
  0.6 103.4 %copy-start.3 = (f32[3,1,8,256]{3,2,1,0:T(8,128)S(1)}, f32[3,1,8,256]{3,2,1,0:T(8,128)}, u32[]{:S(2)}) copy-start(f32[3,1,8,256]{3,2,1,0:T(8,128)} %param.13) | copy-start | bytes 73732
  0.7 103.4 %copy-start.1 = (f32[3,8,1,8,256]{4,3,2,1,0:T(8,128)S(1)}, f32[3,8,1,8,256]{4,3,2,1,0:T(8,128)}, u32[]{:S(2)}) copy-start(f32[3,8,1,8,256]{4,3,2,1,0:T(8,128)} %param.12) | copy-start | bytes 589828
  0.7 102.6 %copy-start.9 = (f32[3,1,256]{2,1,0:T(1,128)S(1)}, f32[3,1,256]{2,1,0:T(1,128)}, u32[]{:S(2)}) copy-start(f32[3,1,256]{2,1,0:T(1,128)} %param.19) | copy-start | bytes 9220
  2.5 101.5 %collective-permute-start.1 = (f32[28,1,8,256]{3,2,1,0:T(8,128)S(1)}, f32[28,1,8,256]{3,2,1,0:T(8,128)S(1)}, u32[]{:S(2)}, u32[]{:S(2)}) collective-permute-start(f32[28,1,8,256]{3,2,1,0:T(8,128)S(1)} %pad_maximum_fusion.1), channel_id=1, source_target_pairs={{4,0},{8,4},{12,8},{16,12},{20,16},{24,20},{28,24},{5,1},{9,5},{13... | collective-permute-start | bytes 688136 | tf_op jit(solution)/shard_map/ppermute | solution.py:17
  3.8 100.3 %collective-permute-start = (f32[28,1,8,256]{3,2,1,0:T(8,128)S(1)}, f32[28,1,8,256]{3,2,1,0:T(8,128)S(1)}, u32[]{:S(2)}, u32[]{:S(2)}) collective-permute-start(f32[28,1,8,256]{3,2,1,0:T(8,128)S(1)} %pad_maximum_fusion.1), channel_id=1, source_target_pairs={{0,4},{4,8},{8,12},{12,16},{16,20},{20,24},{24,28},{1,5},{5,9},{9,... | collective-permute-start | bytes 688136 | tf_op jit(solution)/shard_map/ppermute | solution.py:16
  51.6 52.2 %all-to-all-start = ((f32[1,64,8]{1,0,2:T(1,128)}), f32[1,64,8]{1,0,2:T(1,128)S(1)}, u32[]{:S(2)}, u32[]{:S(2)}) async-start(f32[1,64,8]{1,0,2:T(1,128)} %bitcast.34), calls=%async_computation | async-start | bytes 8192 | tf_op jit(solution)/shard_map/all_to_all | solution.py:179
  102.5 0.6 copy-start.6
  104.2 4.1 %collective-permute-start.2 = (f32[28,3,1,256]{3,2,1,0:T(1,128)S(1)}, f32[28,3,1,256]{3,2,1,0:T(1,128)S(1)}, u32[]{:S(2)}, u32[]{:S(2)}) collective-permute-start(f32[28,3,1,256]{3,2,1,0:T(1,128)S(1)} %get-tuple-element.45), channel_id=1, source_target_pairs={{0,1},{1,2},{2,3},{4,5},{5,6},{6,7},{8,9},{9,10},{10,11},{12,13},{... | collective-permute-start | bytes 258056 | tf_op jit(solution)/shard_map/ppermute | solution.py:16
  106.5 3.2 %collective-permute-start.3 = (f32[28,3,1,256]{3,2,1,0:T(1,128)S(1)}, f32[28,3,1,256]{3,2,1,0:T(1,128)S(1)}, u32[]{:S(2)}, u32[]{:S(2)}) collective-permute-start(f32[28,3,1,256]{3,2,1,0:T(1,128)S(1)} %get-tuple-element.46), channel_id=1, source_target_pairs={{1,0},{2,1},{3,2},{5,4},{6,5},{7,6},{9,8},{10,9},{11,10},{13,12},{... | collective-permute-start | bytes 258056 | tf_op jit(solution)/shard_map/ppermute | solution.py:17
  128.3 5.2 %copy-start.5 = (f32[2,9,256]{2,1,0:T(8,128)S(1)}, f32[2,9,256]{2,1,0:T(8,128)}, u32[]{:S(2)}) copy-start(f32[2,9,256]{2,1,0:T(8,128)} %slice.139) | copy-start | bytes 55300
  133.5 3.7 %copy-start.2 = (f32[3,8,1,8,256]{4,3,2,1,0:T(8,128)S(1)}, f32[3,8,1,8,256]{4,3,2,1,0:T(8,128)}, u32[]{:S(2)}) copy-start(f32[3,8,1,8,256]{4,3,2,1,0:T(8,128)} %param.12) | copy-start | bytes 589828
  133.5 3.7 %copy-start.4 = (f32[3,1,8,256]{3,2,1,0:T(8,128)S(1)}, f32[3,1,8,256]{3,2,1,0:T(8,128)}, u32[]{:S(2)}) copy-start(f32[3,1,8,256]{3,2,1,0:T(8,128)} %param.13) | copy-start | bytes 73732
  133.5 3.7 %copy-start.7 = (f32[1,3,8]{2,1,0:T(4,128)S(1)}, f32[1,3,8]{2,1,0:T(4,128)}, u32[]{:S(2)}) copy-start(f32[1,3,8]{2,1,0:T(4,128)} %copy-done.6) | copy-start | bytes 292
  137.2 37.9 %copy-start.8 = (f32[3,1,256]{2,0,1:T(4,128)S(1)}, f32[3,1,256]{2,0,1:T(4,128)}, u32[]{:S(2)}) copy-start(f32[3,1,256]{2,0,1:T(4,128)} %copy.121) | copy-start | bytes 9220
  195.1 11.1 %all-to-all-start.1 = ((f32[8,1,512]{2,1,0:T(1,128)}), f32[8,1,512]{2,1,0:T(1,128)S(1)}, u32[]{:S(2)}, u32[]{:S(2)}) async-start(f32[8,1,512]{2,1,0:T(1,128)} %reshape.504), calls=%async_computation.1 | async-start | bytes 32768 | tf_op jit(solution)/shard_map/all_to_all | solution.py:178
